TPU v7x, 32 devices: a whole 2x2x4 slice. The times are simulated.
32 devices in a mesh: chan: 8 (over y, x, core), stn: 4 (over z).
Axes of the slice: x: 2, y: 2, z: 4, core: 2. Of those that a mesh axis runs over, the one named last changes fastest.
Arguments:
- measured_correlation: float32 [8, 8, 4096], P('chan', None, 'stn'), may hold values from -3 to 3
- model_correlation: float32 [8, 8, 16, 4096], P('chan', None, None, 'stn'), may hold values from -1.0606601 to 1.0606601
- source_pointing: int32 [16, 1], replicated, may hold values from 0 to 7
- antenna_pairs: int32 [2, 4096], P(None, 'stn'), may hold values from 0 to 511, as said below
- starting_jones_matrices: float32 [8, 8, 8, 512], P('chan'), may hold values from -1 to 2
- starting_polynomial_terms: float32 [3, 8, 8, 512], replicated, may hold values from -1 to 2
- starting_lagrange_scaled: float32 [8, 8, 8, 512], P('chan'), may hold values from -1.5 to 1.5
- augmented_lagrange_rhos: float32 [8], replicated, may hold values from 0.5 to 4
Outputs:
- solved_gains: float32 [8, 8, 8, 512], P('chan', None, None, 'stn')
- solved_dual: float32 [8, 8, 8, 512], P('chan', None, None, 'stn')
- fit_coeffs: float32 [3, 8, 8, 512], P(None, None, None, 'stn')
Inputs may be any that keep to these rules, and one draw needn't show every extreme that they name: `antenna_pairs`: row 0 holds a baseline's first station and row 1 its second, which differs from the first. The first station of every baseline in the i-th aligned block of 1024 baselines lies among stations i * 128 to (i + 1) * 128 - 1. `source_pointing`: every direction holds at least one component.
All inputs are finite; a program needn't handle non-finite values.
Results may differ from a plain program's by a relative error of at most 0.0001.
Values sent between devices are 32-bit elements; how exact they have to be, the bound alone decides.
No kernel may reach another device: no remote copies, remote signals or barrier semaphores. Data moves between devices by JAX's collectives and lax.ppermute only.
A program may use at most 64 MiB of HBM per device.

v0:
```python
from functools import partial
import jax
import jax.numpy as jnp
from jax import lax
from jax.sharding import PartitionSpec as P

CALIB_PATHS = 8
TERMS = 3
STEPS = 2
INNER = 2
student_nu = 2.0
squared_tolerance = 1e-06
highest = lax.Precision.HIGHEST


def entries(stacked):
    return [(stacked[slot_idx], stacked[4 + slot_idx]) for slot_idx in range(4)]


def assemble(matrix):
    return jnp.stack(
        [matrix[slot_idx][0] for slot_idx in range(4)]
        + [matrix[slot_idx][1] for slot_idx in range(4)],
        axis=0,
    )


def flatten(matrix):
    return [matrix[slot_idx][0] for slot_idx in range(4)] + [
        matrix[slot_idx][1] for slot_idx in range(4)
    ]


def multiply_pair(first_pair, second_pair):
    return (
        first_pair[0] * second_pair[0] - first_pair[1] * second_pair[1],
        first_pair[0] * second_pair[1] + first_pair[1] * second_pair[0],
    )


def add_pair(first_pair, second_pair):
    return (first_pair[0] + second_pair[0], first_pair[1] + second_pair[1])


def conjugate(value_pair):
    return (value_pair[0], -value_pair[1])


def matrix_product(factor_one, factor_two):
    return [
        add_pair(
            multiply_pair(factor_one[0], factor_two[0]), multiply_pair(factor_one[1], factor_two[2])
        ),
        add_pair(
            multiply_pair(factor_one[0], factor_two[1]), multiply_pair(factor_one[1], factor_two[3])
        ),
        add_pair(
            multiply_pair(factor_one[2], factor_two[0]), multiply_pair(factor_one[3], factor_two[2])
        ),
        add_pair(
            multiply_pair(factor_one[2], factor_two[1]), multiply_pair(factor_one[3], factor_two[3])
        ),
    ]


def adjoint(matrix):
    return [conjugate(matrix[0]), conjugate(matrix[2]), conjugate(matrix[1]), conjugate(matrix[3])]


def gram_parts(matrix):
    upper_sum = (
        matrix[0][0] * matrix[0][0]
        + matrix[0][1] * matrix[0][1]
        + matrix[1][0] * matrix[1][0]
        + matrix[1][1] * matrix[1][1]
    )
    lower_sum = (
        matrix[2][0] * matrix[2][0]
        + matrix[2][1] * matrix[2][1]
        + matrix[3][0] * matrix[3][0]
        + matrix[3][1] * matrix[3][1]
    )
    cross_term = add_pair(
        multiply_pair(matrix[0], conjugate(matrix[2])),
        multiply_pair(matrix[1], conjugate(matrix[3])),
    )
    return [upper_sum, lower_sum, cross_term[0], cross_term[1]]


def basis_table(channel_count):
    frequency = (2.0 * jnp.arange(channel_count, dtype=jnp.float32) + 1.0) / channel_count - 1.0
    columns = []
    for degree in range(TERMS):
        column = frequency**degree
        for earlier in columns:
            column = column - jnp.sum(earlier * column) / channel_count * earlier
        column = column / jnp.sqrt(jnp.sum(column * column) / channel_count)
        columns.append(column)
    return jnp.stack(columns, axis=1)


def combine_sources(cohere_f, source_pointing):
    member = (
        source_pointing[:, 0][:, None] == jnp.arange(CALIB_PATHS, dtype=jnp.int32)[None, :]
    ).astype(jnp.float32)
    return jnp.einsum("csb,sk->ckb", cohere_f, member, precision=highest)


def channel_state(vis_f, cohere_dir, spectral_jones_matrices, antenna_pairs):
    coherent = entries(cohere_dir)
    first_gain = entries(spectral_jones_matrices[:, :, antenna_pairs[0]])
    second_gain = entries(spectral_jones_matrices[:, :, antenna_pairs[1]])
    toward_first = matrix_product(coherent, adjoint(second_gain))
    own_terms = matrix_product(first_gain, toward_first)
    observed = entries(vis_f)
    residual = [
        (
            observed[slot_idx][0] - jnp.sum(own_terms[slot_idx][0], axis=0),
            observed[slot_idx][1] - jnp.sum(own_terms[slot_idx][1], axis=0),
        )
        for slot_idx in range(4)
    ]
    energy = residual[0][0] * residual[0][0] + residual[0][1] * residual[0][1]
    for slot_idx in range(1, 4):
        energy = (
            energy
            + residual[slot_idx][0] * residual[slot_idx][0]
            + residual[slot_idx][1] * residual[slot_idx][1]
        )
    return (residual, own_terms, toward_first, first_gain, coherent, energy)


def channel_sums(chan_state, weight, first_table, second_table, block_start):
    residual, own_terms, toward_first, first_gain, coherent, energy = chan_state
    target = [
        add_pair((residual[slot_idx][0][None], residual[slot_idx][1][None]), own_terms[slot_idx])
        for slot_idx in range(4)
    ]
    back_terms = matrix_product(first_gain, coherent)
    first_parts = (
        jnp.stack(
            gram_parts(toward_first) + flatten(matrix_product(target, adjoint(toward_first))),
            axis=0,
        )
        * weight
    )
    second_parts = (
        jnp.stack(
            gram_parts(adjoint(back_terms)) + flatten(matrix_product(adjoint(target), back_terms)),
            axis=0,
        )
        * weight
    )
    first_block = jnp.einsum("pkb,bs->pks", first_parts, first_table, precision=highest)
    every_station = jnp.einsum("pkb,bs->pks", second_parts, second_table, precision=highest)
    block_width = first_table.shape[1]
    own_rows = lax.dynamic_slice_in_dim(every_station, block_start, block_width, 2) + first_block
    return lax.dynamic_update_slice_in_dim(every_station, own_rows, block_start, 2)


def jones_estimator(
    least_squares_equations, pivot_spectral_point, spectral_jones_matrices, augmented_lagrange_rhos
):
    augmented_rho_factor = augmented_lagrange_rhos[:, None]
    diag_one = least_squares_equations[0] + augmented_rho_factor
    diag_two = least_squares_equations[1] + augmented_rho_factor
    determinant = (
        diag_one * diag_two
        - least_squares_equations[2] * least_squares_equations[2]
        - least_squares_equations[3] * least_squares_equations[3]
    )
    zero_part = jnp.zeros_like(determinant)
    inverse = [
        (diag_two / determinant, zero_part),
        (-least_squares_equations[2] / determinant, -least_squares_equations[3] / determinant),
        (-least_squares_equations[2] / determinant, least_squares_equations[3] / determinant),
        (diag_one / determinant, zero_part),
    ]
    right_side = entries(
        least_squares_equations[4:] + augmented_rho_factor[None] * pivot_spectral_point
    )
    solution = assemble(matrix_product(right_side, inverse))
    return 0.5 * (spectral_jones_matrices + solution)


def body(
    measured_correlation,
    model_correlation,
    source_pointing,
    antenna_pairs,
    starting_jones_matrices,
    starting_polynomial_terms,
    starting_lagrange_scaled,
    augmented_lagrange_rhos,
):
    local_ch = measured_correlation.shape[0]
    stations = starting_jones_matrices.shape[3]
    block_size = stations // lax.axis_size("stn")
    block_start = lax.axis_index("stn") * block_size
    total_ch = local_ch * lax.axis_size("chan")
    sample_count = total_ch * measured_correlation.shape[2] * lax.axis_size("stn")
    my_basis = lax.dynamic_slice_in_dim(
        basis_table(total_ch), lax.axis_index("chan") * local_ch, local_ch, 0
    )
    cohere_dir = jax.vmap(combine_sources, (0, None))(model_correlation, source_pointing)
    first_table = (
        (antenna_pairs[0] - block_start)[:, None]
        == jnp.arange(block_size, dtype=jnp.int32)[None, :]
    ).astype(jnp.float32)
    second_table = (
        antenna_pairs[1][:, None] == jnp.arange(stations, dtype=jnp.int32)[None, :]
    ).astype(jnp.float32)
    state_fn = jax.vmap(channel_state, (0, 0, 0, None))
    sums_fn = jax.vmap(
        partial(
            channel_sums,
            first_table=first_table,
            second_table=second_table,
            block_start=block_start,
        ),
        (0, 0),
    )
    estimate_routine = jax.vmap(jones_estimator, (0, 0, 0, None))

    def own_block(array):
        return lax.dynamic_slice_in_dim(array, block_start, block_size, 3)

    consensus = jnp.einsum("ft,tcks->fcks", my_basis, starting_polynomial_terms, precision=highest)
    whole_jones_matrix = starting_jones_matrices
    dual_now = starting_lagrange_scaled
    gain_mine = starting_jones_matrices
    pending = None
    fit_now = starting_polynomial_terms
    for step_idx in range(STEPS):
        pivot_antenna = consensus - dual_now
        for inner_idx in range(INNER):
            chan_state = state_fn(
                measured_correlation, cohere_dir, whole_jones_matrix, antenna_pairs
            )
            mean_square = (
                lax.psum(jnp.sum(chan_state[5]), ("chan", "stn")) / sample_count + squared_tolerance
            )
            weight = (student_nu + 2.0) / (student_nu + chan_state[5] / mean_square)
            least_squares_equations = sums_fn(chan_state, weight)
            whole_accumulated_totals = lax.psum(least_squares_equations, "stn")
            whole_jones_matrix = estimate_routine(
                whole_accumulated_totals, pivot_antenna, whole_jones_matrix, augmented_lagrange_rhos
            )
            gain_mine = whole_jones_matrix
        partial_fit = jnp.einsum("ft,fcks->tcks", my_basis, gain_mine + dual_now, precision=highest)
        fit_now = lax.psum(partial_fit, "chan") / total_ch
        consensus = jnp.einsum("ft,tcks->fcks", my_basis, fit_now, precision=highest)
        dual_now = dual_now + gain_mine - consensus
    return (own_block(gain_mine), own_block(dual_now), own_block(fit_now))


def solution(mesh):
    placed = (
        P("chan", None, "stn"),
        P("chan", None, None, "stn"),
        P(),
        P(None, "stn"),
        P("chan", None, None, None),
        P(),
        P("chan", None, None, None),
        P(),
    )
    return jax.shard_map(
        body,
        mesh=mesh,
        in_specs=placed,
        out_specs=(
            P("chan", None, None, "stn"),
            P("chan", None, None, "stn"),
            P(None, None, None, "stn"),
        ),
        check_vma=False,
    )
```

profile of v0, /device:TPU:0, one launch (start us, length us, event | category | flops | bytes accessed | tf_op | source)
XLA Modules:
  0.0 534.8 jit_solution(3968500334893282561)
XLA Ops:
  10.2 1.0 fusion.296
  11.2 1.7 copy.196
  12.9 9.1 %gather_fusion.1 = f32[1024,8,8]{2,1,0:T(8,128)} fusion(f32[8,8,512]{1,0,2:T(8,128)S(1)} %bitcast.987, s32[1024]{0:T(1024)S(1)} %get-tuple-element.362), kind=kCustom, calls=%fused_computation.1 | custom fusion | bytes 528384 | tf_op jit(solution)/shard_map/vmap()/gather | solution.py:112
  21.9 2.8 copy.209
  24.7 9.1 %gather_fusion = f32[1024,8,8]{2,1,0:T(8,128)} fusion(f32[8,8,512]{1,0,2:T(8,128)S(1)} %bitcast.988, s32[1024]{0:T(1024)S(1)} %get-tuple-element.363), kind=kCustom, calls=%fused_computation | custom fusion | bytes 528384 | tf_op jit(solution)/shard_map/vmap()/gather | solution.py:111
  33.8 2.8 copy.197
  38.6 42.2 %psum.70 = f32[]{:T(128)} all-reduce(f32[]{:T(128)} %fusion.207), channel_id=1, replica_groups=mesh['chan'=8,'stn'=4] {'chan','stn'}, use_global_device_ids=true, to_apply=%region_9.0 | all-reduce | flops 1 | bytes 8 | tf_op jit(solution)/shard_map/psum | solution.py:241
  82.9 1.9 fusion.7
  84.9 2.3 fusion.16
  87.2 1.0 scatter.14
  95.5 1.2 fusion.27
  96.7 27.4 %all-reduce.8.cloned.1.call-done = f32[1,12,8,512]{3,2,1,0:T(8,128)} async-done(((f32[1,12,8,512]{3,2,1,0:T(8,128)}), f32[1,12,8,512]{3,2,1,0:T(8,128)}) %all-reduce.8.cloned.1.call-update) | async-done | bytes 196624 | tf_op jit(solution)/shard_map/psum | solution.py:245
  124.0 1.0 slice_add_fusion.3
  127.5 1.7 copy.236
  129.1 9.1 %gather_fusion.3 = f32[1024,8,8]{2,1,0:T(8,128)} fusion(f32[8,8,512]{1,0,2:T(8,128)S(1)} %copy.236, s32[1024]{0:T(1024)S(1)} %get-tuple-element.362), kind=kCustom, calls=%fused_computation.3 | custom fusion | bytes 528384 | tf_op jit(solution)/shard_map/vmap()/gather | solution.py:112
  138.2 9.1 %gather_fusion.2 = f32[1024,8,8]{2,1,0:T(8,128)} fusion(f32[8,8,512]{1,0,2:T(8,128)S(1)} %copy.236, s32[1024]{0:T(1024)S(1)} %get-tuple-element.363), kind=kCustom, calls=%fused_computation.2 | custom fusion | bytes 528384 | tf_op jit(solution)/shard_map/vmap()/gather | solution.py:111
  147.3 2.8 copy.243
  150.2 2.8 copy.237
  153.9 40.5 %psum.72 = f32[]{:T(128)} all-reduce(f32[]{:T(128)} %fusion.206), channel_id=1, replica_groups=mesh['chan'=8,'stn'=4] {'chan','stn'}, use_global_device_ids=true, to_apply=%region_26.0 | all-reduce | flops 1 | bytes 8 | tf_op jit(solution)/shard_map/psum | solution.py:241
  195.8 1.0 fusion.5
  196.8 2.3 fusion.14
  199.1 1.0 scatter.15
  200.9 34.9 %all-reduce.10.cloned.1.call-done = f32[1,12,8,512]{3,2,0,1:T(8,128)} async-done(((f32[1,12,8,512]{3,2,0,1:T(8,128)}), f32[1,12,8,512]{3,2,0,1:T(8,128)}) %all-reduce.10.cloned.1.call-update) | async-done | bytes 196624 | tf_op jit(solution)/shard_map/psum | solution.py:245
  235.8 1.0 slice_add_fusion.2
  239.4 9.1 %gather_fusion.5 = f32[1024,8,8]{2,1,0:T(8,128)} fusion(f32[8,8,512]{1,0,2:T(8,128)S(1)} %copy.249, s32[1024]{0:T(1024)S(1)} %get-tuple-element.362), kind=kCustom, calls=%fused_computation.5 | custom fusion | bytes 528384 | tf_op jit(solution)/shard_map/vmap()/gather | solution.py:112
  248.5 9.1 %gather_fusion.4 = f32[1024,8,8]{2,1,0:T(8,128)} fusion(f32[8,8,512]{1,0,2:T(8,128)S(1)} %copy.249, s32[1024]{0:T(1024)S(1)} %get-tuple-element.363), kind=kCustom, calls=%fused_computation.4 | custom fusion | bytes 528384 | tf_op jit(solution)/shard_map/vmap()/gather | solution.py:111
  257.5 2.8 copy.256
  260.5 2.8 copy.250
  265.1 40.3 %psum.74 = f32[]{:T(128)} all-reduce(f32[]{:T(128)} %fusion.205), channel_id=1, replica_groups=mesh['chan'=8,'stn'=4] {'chan','stn'}, use_global_device_ids=true, to_apply=%region_37.0 | all-reduce | flops 1 | bytes 8 | tf_op jit(solution)/shard_map/psum | solution.py:241
  307.8 2.3 fusion.12
  310.1 1.0 scatter.16
  312.1 7.3 %all-reduce.14.cloned.1.call-done = f32[3,8,8,512]{3,2,1,0:T(8,128)} async-done(((f32[3,8,8,512]{3,2,1,0:T(8,128)}), f32[3,8,8,512]{3,2,1,0:T(8,128)}) %all-reduce.14.cloned.1.call-update) | async-done | bytes 393232 | tf_op jit(solution)/shard_map/psum | solution.py:251
  319.3 1.0 broadcast_multiply_fusion.2
  320.3 1.2 fusion.25
  321.5 34.4 %all-reduce.12.cloned.1.call-done = f32[1,12,8,512]{3,2,0,1:T(8,128)} async-done(((f32[1,12,8,512]{3,2,0,1:T(8,128)}), f32[1,12,8,512]{3,2,0,1:T(8,128)}) %all-reduce.12.cloned.1.call-update) | async-done | bytes 196624 | tf_op jit(solution)/shard_map/psum | solution.py:245
  355.9 1.0 slice_add_fusion.1
  360.0 9.1 %gather_fusion.7 = f32[1024,8,8]{2,1,0:T(8,128)} fusion(f32[8,8,512]{1,0,2:T(8,128)S(1)} %copy.264, s32[1024]{0:T(1024)S(1)} %get-tuple-element.362), kind=kCustom, calls=%fused_computation.7 | custom fusion | bytes 528384 | tf_op jit(solution)/shard_map/vmap()/gather | solution.py:112
  369.2 9.1 %gather_fusion.6 = f32[1024,8,8]{2,1,0:T(8,128)} fusion(f32[8,8,512]{1,0,2:T(8,128)S(1)} %copy.264, s32[1024]{0:T(1024)S(1)} %get-tuple-element.363), kind=kCustom, calls=%fused_computation.6 | custom fusion | bytes 528384 | tf_op jit(solution)/shard_map/vmap()/gather | solution.py:111
  378.2 2.8 copy.271
  381.1 2.8 copy.265
  384.9 40.3 %psum.77 = f32[]{:T(128)} all-reduce(f32[]{:T(128)} %fusion.204), channel_id=1, replica_groups=mesh['chan'=8,'stn'=4] {'chan','stn'}, use_global_device_ids=true, to_apply=%region_49.0 | all-reduce | flops 1 | bytes 8 | tf_op jit(solution)/shard_map/psum | solution.py:241
  427.5 2.3 fusion.10
  429.9 1.0 scatter.19
  431.6 34.9 %all-reduce.16.cloned.1.call-done = f32[1,12,8,512]{3,2,0,1:T(8,128)} async-done(((f32[1,12,8,512]{3,2,0,1:T(8,128)}), f32[1,12,8,512]{3,2,0,1:T(8,128)}) %all-reduce.16.cloned.1.call-update) | async-done | bytes 196624 | tf_op jit(solution)/shard_map/psum | solution.py:245
  466.5 1.0 slice_add_fusion
  470.9 53.6 %all-reduce.18.cloned.1.call-done = f32[3,8,8,512]{3,2,1,0:T(8,128)} async-done(((f32[3,8,8,512]{3,2,1,0:T(8,128)}), f32[3,8,8,512]{3,2,1,0:T(8,128)}) %all-reduce.18.cloned.1.call-update) | async-done | bytes 393232 | tf_op jit(solution)/shard_map/psum | solution.py:251
  524.5 1.0 broadcast_multiply_fusion.1
  526.2 1.1 fusion.23
  (229 shorter events, 33.0 us)
Async XLA Ops:
  7.2 29.5 %copy-start = (f32[1,8,16,1024]{3,2,1,0:T(8,128)S(1)}, f32[1,8,16,1024]{3,2,1,0:T(8,128)}, u32[]{:S(2)}) copy-start(f32[1,8,16,1024]{3,2,1,0:T(8,128)} %param.17) | copy-start | bytes 1572868
  7.2 116.8 %all-reduce.8.cloned.1.call-start = ((), (), s32[]{:S(2)}) async-start(), calls=%async_computation | async-start | bytes 393216 | tf_op jit(solution)/shard_map/psum | solution.py:245
  21.9 14.7 %copy-start.17 = (s32[16,1]{0,1:T(1,128)S(1)}, s32[16,1]{0,1:T(1,128)}, u32[]{:S(2)}) copy-start(s32[16,1]{0,1:T(1,128)} %param.18) | copy-start | bytes 196
  33.8 3.5 copy-start.1
  37.1 44.4 %copy-start.16 = (s32[4]{0:T(128)S(1)}, s32[4]{0:T(128)}, u32[]{:S(2)}) copy-start(s32[4]{0:T(128)} %constant.139.clone.1) | copy-start | bytes 52
  37.3 58.2 %copy-start.7 = (f32[3,8,8,512]{3,2,1,0:T(8,128)S(1)}, f32[3,8,8,512]{3,2,1,0:T(8,128)}, u32[]{:S(2)}) copy-start(f32[3,8,8,512]{3,2,1,0:T(8,128)} %param.21) | copy-start | bytes 1179652
  80.8 43.2 %copy-start.5 = (f32[1,8,8,512]{3,2,1,0:T(8,128)S(1)}, f32[1,8,8,512]{3,2,1,0:T(8,128)}, u32[]{:S(2)}) copy-start(f32[1,8,8,512]{3,2,1,0:T(8,128)} %param.22) | copy-start | bytes 393220
  80.8 43.2 %copy-start.14 = (f32[8]{0:T(128)S(1)}, f32[8]{0:T(128)}, u32[]{:S(2)}) copy-start(f32[8]{0:T(128)} %param.23) | copy-start | bytes 100
  81.1 45.7 %copy-start.6 = (f32[1,8,8,512]{3,2,1,0:T(8,128)S(1)}, f32[1,8,8,512]{3,2,1,0:T(8,128)}, u32[]{:S(2)}) copy-start(f32[1,8,8,512]{3,2,1,0:T(8,128)} %param.20) | copy-start | bytes 393220
  81.5 1.4 copy-start.15
  88.2 0.7 copy-start.12
  88.9 146.9 %all-reduce.10.cloned.1.call-start = ((), (), s32[]{:S(2)}) async-start(), calls=%async_computation.1 | async-start | bytes 393216 | tf_op jit(solution)/shard_map/psum | solution.py:245
  200.1 0.7 copy-start.13
  200.8 118.5 %all-reduce.14.cloned.1.call-start = ((), (), s32[]{:S(2)}) async-start(), calls=%async_computation.3 | async-start | bytes 786432 | tf_op jit(solution)/shard_map/psum | solution.py:251
  238.6 9.9 %copy-start.2 = (f32[1,8,8,512]{3,2,1,0:T(8,128)}, f32[1,8,8,512]{3,2,1,0:T(8,128)S(1)}, u32[]{:S(2)}) copy-start(f32[1,8,8,512]{3,2,1,0:T(8,128)S(1)} %get-tuple-element.150) | copy-start | bytes 393220
  265.0 90.8 %all-reduce.12.cloned.1.call-start = ((), (), s32[]{:S(2)}) async-start(), calls=%async_computation.2 | async-start | bytes 393216 | tf_op jit(solution)/shard_map/psum | solution.py:245
  306.4 52.8 %copy-start.3 = (f32[1,8,8,512]{3,2,1,0:T(8,128)S(1)}, f32[1,8,8,512]{3,2,1,0:T(8,128)}, u32[]{:S(2)}) copy-start(f32[1,8,8,512]{3,2,1,0:T(8,128)} %copy-done.2) | copy-start | bytes 393220
  311.1 0.7 copy-start.10
  311.8 154.7 %all-reduce.16.cloned.1.call-start = ((), (), s32[]{:S(2)}) async-start(), calls=%async_computation.4 | async-start | bytes 393216 | tf_op jit(solution)/shard_map/psum | solution.py:245
  358.6 0.6 copy-start.8
  426.0 43.3 %copy-start.4 = (f32[1,8,8,512]{3,2,1,0:T(8,128)S(1)}, f32[1,8,8,512]{3,2,1,0:T(8,128)}, u32[]{:S(2)}) copy-start(f32[1,8,8,512]{3,2,1,0:T(8,128)} %copy-done.2) | copy-start | bytes 393220
  426.0 43.3 %copy-start.9 = (f32[8,1,8,512]{3,2,0,1:T(8,128)S(1)}, f32[8,1,8,512]{3,2,0,1:T(8,128)}, u32[]{:S(2)}) copy-start(f32[8,1,8,512]{3,2,0,1:T(8,128)} %copy-done.8) | copy-start | bytes 393220
  430.9 0.7 copy-start.11
  431.6 92.9 %all-reduce.18.cloned.1.call-start = ((), (), s32[]{:S(2)}) async-start(), calls=%async_computation.5 | async-start | bytes 786432 | tf_op jit(solution)/shard_map/psum | solution.py:251
Sparse Core Ops, SparseCore 0:
  89.0 34.9 all-reduce.7
  200.9 34.8 all-reduce.9
  265.2 54.1 all-reduce.13
  321.5 34.3 all-reduce.11
  431.7 34.8 all-reduce.15
  470.4 54.0 all-reduce.17
where the time goes:
time: 538 us; the launch traced here: 535 us
  waiting for transfers between devices  192 us (36%)
  blocking collectives  163 us (30%)
  local copies, waits for them, and re-layouts  111 us (21%)
  other arithmetic  28.8 us (5%)
  between operations  21.2 us (4%)
  matrix products  17.9 us (3%)
    psum x4, blocking collectives, body(): lax.psum(jnp.sum(chan_state[5]), ('chan', 'stn')) / sample_count  163 us
    psum x4, waiting for transfers between devices, body(): whole_accumulated_totals = lax.psum(least_squares_equations, 'stn')  132 us
    psum x2, waiting for transfers between devices, body(): fit_now = lax.psum(partial_fit, 'chan') / total_ch  60.8 us
    gather x8, local copies, waits for them, and re-layouts, channel_state(): second_gain = entries(spectral_jones_matrices[:, :, antenna_pairs[1]])  47.6 us
    gather x8, local copies, waits for them, and re-layouts, channel_state(): first_gain = entries(spectral_jones_matrices[:, :, antenna_pairs[0]])  47.5 us
  transfers between devices with their start and end apart: 6, of which 6 were waited for; matrix products, arithmetic and copies ran while one was open for 2% of the time, Pallas kernels for 0%

commit v1 on v0

--- a/solution.py
+++ b/solution.py
@@ -242,7 +242,9 @@
             )
             weight = (student_nu + 2.0) / (student_nu + chan_state[5] / mean_square)
             least_squares_equations = sums_fn(chan_state, weight)
-            whole_accumulated_totals = lax.psum(least_squares_equations, "stn")
+            whole_accumulated_totals = jnp.sum(
+                lax.all_gather(least_squares_equations, "stn"), axis=0
+            )
             whole_jones_matrix = estimate_routine(
                 whole_accumulated_totals, pivot_antenna, whole_jones_matrix, augmented_lagrange_rhos
             )

time: 538 us -> 455 us (0.85)
  waiting for transfers between devices: 192 us -> 55.1 us
  blocking collectives: 163 us -> 233 us
  other arithmetic: 28.8 us -> 20 us
    psum x4 -> x0, waiting for transfers between devices: 132 us -> none  [body(): whole_accumulated_totals = lax.psum(least_squares_equations, 'stn')]
    all_gather x0 -> x4, blocking collectives: none -> 72.8 us  [body(): lax.all_gather(least_squares_equations, 'stn')]
    psum x2, waiting for transfers between devices: 60.8 us -> 55.1 us  [body(): fit_now = lax.psum(partial_fit, 'chan') / total_ch]
    unnamed x113, other arithmetic: 9.72 us -> 4.31 us
  transfers between devices with their start and end apart: 6 -> 2, of which waited for: 6 -> 1; matrix products, arithmetic and copies ran while one was open for 2% -> 7% of each run, Pallas kernels for 0% -> 0%
where the time goes in v1:
time: 455 us; the launch traced here: 454 us
  blocking collectives  233 us (51%)
  local copies, waits for them, and re-layouts  108 us (24%)
  waiting for transfers between devices  55.1 us (12%)
  between operations  21.1 us (5%)
  other arithmetic  20 us (4%)
  matrix products  17 us (4%)
    psum x4, blocking collectives, body(): lax.psum(jnp.sum(chan_state[5]), ('chan', 'stn')) / sample_count  160 us
    all_gather x4, blocking collectives, body(): lax.all_gather(least_squares_equations, 'stn')  72.8 us
    psum x2, waiting for transfers between devices, body(): fit_now = lax.psum(partial_fit, 'chan') / total_ch  55.1 us
    gather x8, local copies, waits for them, and re-layouts, channel_state(): second_gain = entries(spectral_jones_matrices[:, :, antenna_pairs[1]])  47.6 us
    gather x8, local copies, waits for them, and re-layouts, channel_state(): first_gain = entries(spectral_jones_matrices[:, :, antenna_pairs[0]])  47.5 us
    dot_general x4, matrix products, channel_sums(): jnp.einsum('pkb,bs->pks', first_parts, first_table, precision=highest)  9.5 us
  transfers between devices with their start and end apart: 2, of which 1 were waited for; matrix products, arithmetic and copies ran while one was open for 7% of the time, Pallas kernels for 0%

profile of v1, /device:TPU:0, one launch (start us, length us, event | category | flops | bytes accessed | tf_op | source)
XLA Modules:
  0.0 454.1 jit_solution(10579202551962642939)
XLA Ops:
  13.6 0.8 compare_select_fusion
  16.6 1.0 fusion.287
  17.6 1.7 copy.767
  19.3 9.1 %gather_fusion.1 = f32[1024,8,8]{2,1,0:T(8,128)} fusion(f32[8,8,512]{1,0,2:T(8,128)S(1)} %bitcast.889, s32[1024]{0:T(1024)S(1)} %get-tuple-element.371), kind=kCustom, calls=%fused_computation.1 | custom fusion | bytes 528384 | tf_op jit(solution)/shard_map/vmap()/gather | solution.py:112
  28.4 2.8 copy.780
  31.2 9.1 %gather_fusion = f32[1024,8,8]{2,1,0:T(8,128)} fusion(f32[8,8,512]{1,0,2:T(8,128)S(1)} %bitcast.890, s32[1024]{0:T(1024)S(1)} %get-tuple-element.372), kind=kCustom, calls=%fused_computation | custom fusion | bytes 528384 | tf_op jit(solution)/shard_map/vmap()/gather | solution.py:111
  40.3 2.8 copy.768
  45.6 42.2 %psum.42 = f32[]{:T(128)} all-reduce(f32[]{:T(128)} %fusion.199), channel_id=1, replica_groups=mesh['chan'=8,'stn'=4] {'chan','stn'}, use_global_device_ids=true, to_apply=%region_9.0 | all-reduce | flops 1 | bytes 8 | tf_op jit(solution)/shard_map/psum | solution.py:241
  89.9 1.0 fusion.7
  90.9 2.4 fusion.16
  93.3 1.0 scatter.14
  94.3 18.1 %all_gather.34 = f32[4,1,12,8,512]{4,3,2,1,0:T(8,128)S(1)} all-gather(f32[1,1,12,8,512]{4,3,2,1,0:T(8,128)S(1)} %scatter.14), channel_id=1, replica_groups=mesh['chan'=8,'stn'=4] {'stn'}, dimensions={0}, use_global_device_ids=true | all-gather | bytes 983040 | tf_op jit(solution)/shard_map/all_gather | solution.py:246
  112.5 1.1 fusion.27
  114.8 1.7 copy.785
  116.4 9.1 %gather_fusion.3 = f32[1024,8,8]{2,1,0:T(8,128)} fusion(f32[8,8,512]{1,0,2:T(8,128)S(1)} %copy.785, s32[1024]{0:T(1024)S(1)} %get-tuple-element.371), kind=kCustom, calls=%fused_computation.3 | custom fusion | bytes 528384 | tf_op jit(solution)/shard_map/vmap()/gather | solution.py:112
  125.5 9.1 %gather_fusion.2 = f32[1024,8,8]{2,1,0:T(8,128)} fusion(f32[8,8,512]{1,0,2:T(8,128)S(1)} %copy.785, s32[1024]{0:T(1024)S(1)} %get-tuple-element.372), kind=kCustom, calls=%fused_computation.2 | custom fusion | bytes 528384 | tf_op jit(solution)/shard_map/vmap()/gather | solution.py:111
  134.6 2.8 copy.792
  137.5 2.8 copy.786
  141.2 38.9 %psum.43 = f32[]{:T(128)} all-reduce(f32[]{:T(128)} %fusion.198), channel_id=1, replica_groups=mesh['chan'=8,'stn'=4] {'chan','stn'}, use_global_device_ids=true, to_apply=%region_26.0 | all-reduce | flops 1 | bytes 8 | tf_op jit(solution)/shard_map/psum | solution.py:241
  181.5 1.0 fusion.5
  182.5 2.4 fusion.14
  184.9 1.0 scatter.15
  185.9 18.2 %all_gather.37 = f32[4,1,12,8,512]{4,3,2,1,0:T(8,128)S(1)} all-gather(f32[1,1,12,8,512]{4,3,2,1,0:T(8,128)S(1)} %scatter.15), channel_id=1, replica_groups=mesh['chan'=8,'stn'=4] {'stn'}, dimensions={0}, use_global_device_ids=true | all-gather | bytes 983040 | tf_op jit(solution)/shard_map/all_gather | solution.py:246
  204.6 0.9 broadcast_multiply_fusion.3
  206.3 9.1 %gather_fusion.5 = f32[1024,8,8]{2,1,0:T(8,128)} fusion(f32[8,8,512]{1,0,2:T(8,128)S(1)} %copy.797, s32[1024]{0:T(1024)S(1)} %get-tuple-element.371), kind=kCustom, calls=%fused_computation.5 | custom fusion | bytes 528384 | tf_op jit(solution)/shard_map/vmap()/gather | solution.py:112
  215.4 9.1 %gather_fusion.4 = f32[1024,8,8]{2,1,0:T(8,128)} fusion(f32[8,8,512]{1,0,2:T(8,128)S(1)} %copy.797, s32[1024]{0:T(1024)S(1)} %get-tuple-element.372), kind=kCustom, calls=%fused_computation.4 | custom fusion | bytes 528384 | tf_op jit(solution)/shard_map/vmap()/gather | solution.py:111
  224.5 2.8 copy.804
  227.4 2.8 copy.798
  231.1 40.0 %psum.44 = f32[]{:T(128)} all-reduce(f32[]{:T(128)} %fusion.197), channel_id=1, replica_groups=mesh['chan'=8,'stn'=4] {'chan','stn'}, use_global_device_ids=true, to_apply=%region_37.0 | all-reduce | flops 1 | bytes 8 | tf_op jit(solution)/shard_map/psum | solution.py:241
  272.5 1.0 fusion.3
  273.5 2.4 fusion.12
  275.8 1.0 scatter.16
  276.8 18.4 %all_gather.40 = f32[4,1,12,8,512]{4,3,2,1,0:T(8,128)S(1)} all-gather(f32[1,1,12,8,512]{4,3,2,1,0:T(8,128)S(1)} %scatter.16), channel_id=1, replica_groups=mesh['chan'=8,'stn'=4] {'stn'}, dimensions={0}, use_global_device_ids=true | all-gather | bytes 983040 | tf_op jit(solution)/shard_map/all_gather | solution.py:246
  295.3 1.0 broadcast_multiply_fusion.2
  296.3 1.2 fusion.25
  299.3 9.1 %gather_fusion.7 = f32[1024,8,8]{2,1,0:T(8,128)} fusion(f32[8,8,512]{1,0,2:T(8,128)S(1)} %copy.809, s32[1024]{0:T(1024)S(1)} %get-tuple-element.371), kind=kCustom, calls=%fused_computation.7 | custom fusion | bytes 528384 | tf_op jit(solution)/shard_map/vmap()/gather | solution.py:112
  308.4 9.1 %gather_fusion.6 = f32[1024,8,8]{2,1,0:T(8,128)} fusion(f32[8,8,512]{1,0,2:T(8,128)S(1)} %copy.809, s32[1024]{0:T(1024)S(1)} %get-tuple-element.372), kind=kCustom, calls=%fused_computation.6 | custom fusion | bytes 528384 | tf_op jit(solution)/shard_map/vmap()/gather | solution.py:111
  317.5 2.8 copy.816
  320.4 2.8 copy.810
  324.1 38.8 %psum.46 = f32[]{:T(128)} all-reduce(f32[]{:T(128)} %fusion.196), channel_id=1, replica_groups=mesh['chan'=8,'stn'=4] {'chan','stn'}, use_global_device_ids=true, to_apply=%region_49.0 | all-reduce | flops 1 | bytes 8 | tf_op jit(solution)/shard_map/psum | solution.py:241
  364.3 1.0 fusion.1
  365.3 2.4 fusion.10
  367.6 1.0 scatter.19
  368.6 18.1 %all_gather.43 = f32[4,1,12,8,512]{4,3,2,1,0:T(8,128)S(1)} all-gather(f32[1,1,12,8,512]{4,3,2,1,0:T(8,128)S(1)} %scatter.19), channel_id=1, replica_groups=mesh['chan'=8,'stn'=4] {'stn'}, dimensions={0}, use_global_device_ids=true | all-gather | bytes 983040 | tf_op jit(solution)/shard_map/all_gather | solution.py:246
  387.2 0.9 broadcast_multiply_fusion
  388.7 55.0 %all-reduce.6.cloned.1.call-done = f32[3,8,8,512]{3,2,1,0:T(8,128)} async-done(((f32[3,8,8,512]{3,2,1,0:T(8,128)}), f32[3,8,8,512]{3,2,1,0:T(8,128)}) %all-reduce.6.cloned.1.call-update) | async-done | bytes 393232 | tf_op jit(solution)/shard_map/psum | solution.py:253
  443.8 1.0 broadcast_multiply_fusion.1
  445.5 1.1 fusion.23
  (217 shorter events, 20.6 us)
Async XLA Ops:
  7.2 35.9 %copy-start = (f32[1,8,16,1024]{3,2,1,0:T(8,128)S(1)}, f32[1,8,16,1024]{3,2,1,0:T(8,128)}, u32[]{:S(2)}) copy-start(f32[1,8,16,1024]{3,2,1,0:T(8,128)} %param.17) | copy-start | bytes 1572868
  7.2 288.1 %all-reduce.4.cloned.1.call-start = ((), (), s32[]{:S(2)}) async-start(), calls=%async_computation | async-start | bytes 786432 | tf_op jit(solution)/shard_map/psum | solution.py:253
  28.4 14.7 %copy-start.13 = (s32[16,1]{0,1:T(1,128)S(1)}, s32[16,1]{0,1:T(1,128)}, u32[]{:S(2)}) copy-start(s32[16,1]{0,1:T(1,128)} %param.18) | copy-start | bytes 196
  40.3 4.1 copy-start.1
  44.1 44.0 %copy-start.11 = (f32[12,1,8,1024]{3,2,0,1:T(8,128)S(1)}, f32[12,1,8,1024]{3,2,0,1:T(8,128)}, u32[]{:S(2)}) copy-start(f32[12,1,8,1024]{3,2,0,1:T(8,128)} %get-tuple-element.279) | copy-start | bytes 1179652
  44.1 44.4 %copy-start.12 = (s32[4]{0:T(128)S(1)}, s32[4]{0:T(128)}, u32[]{:S(2)}) copy-start(s32[4]{0:T(128)} %constant.143.clone.1) | copy-start | bytes 52
  88.0 24.6 %copy-start.7 = (f32[3,8,8,512]{3,2,1,0:T(8,128)S(1)}, f32[3,8,8,512]{3,2,1,0:T(8,128)}, u32[]{:S(2)}) copy-start(f32[3,8,8,512]{3,2,1,0:T(8,128)} %param.21) | copy-start | bytes 1179652
  88.1 25.7 %copy-start.5 = (f32[1,8,8,512]{3,2,1,0:T(8,128)S(1)}, f32[1,8,8,512]{3,2,1,0:T(8,128)}, u32[]{:S(2)}) copy-start(f32[1,8,8,512]{3,2,1,0:T(8,128)} %param.22) | copy-start | bytes 393220
  88.1 25.7 %copy-start.10 = (f32[8]{0:T(128)S(1)}, f32[8]{0:T(128)}, u32[]{:S(2)}) copy-start(f32[8]{0:T(128)} %param.23) | copy-start | bytes 100
  88.3 25.8 %copy-start.6 = (f32[1,8,8,512]{3,2,1,0:T(8,128)S(1)}, f32[1,8,8,512]{3,2,1,0:T(8,128)}, u32[]{:S(2)}) copy-start(f32[1,8,8,512]{3,2,1,0:T(8,128)} %param.20) | copy-start | bytes 393220
  204.5 10.8 %copy-start.2 = (f32[1,8,8,512]{3,2,1,0:T(8,128)}, f32[1,8,8,512]{3,2,1,0:T(8,128)S(1)}, u32[]{:S(2)}) copy-start(f32[1,8,8,512]{3,2,1,0:T(8,128)S(1)} %get-tuple-element.159) | copy-start | bytes 393220
  205.5 238.3 %all-reduce.6.cloned.1.call-start = ((), (), s32[]{:S(2)}) async-start(), calls=%async_computation.1 | async-start | bytes 786432 | tf_op jit(solution)/shard_map/psum | solution.py:253
  272.3 26.2 %copy-start.3 = (f32[1,8,8,512]{3,2,1,0:T(8,128)S(1)}, f32[1,8,8,512]{3,2,1,0:T(8,128)}, u32[]{:S(2)}) copy-start(f32[1,8,8,512]{3,2,1,0:T(8,128)} %copy-done.2) | copy-start | bytes 393220
  297.8 0.7 copy-start.8
  363.9 23.2 %copy-start.4 = (f32[1,8,8,512]{3,2,1,0:T(8,128)S(1)}, f32[1,8,8,512]{3,2,1,0:T(8,128)}, u32[]{:S(2)}) copy-start(f32[1,8,8,512]{3,2,1,0:T(8,128)} %copy-done.2) | copy-start | bytes 393220
  363.9 23.2 %copy-start.9 = (f32[8,1,8,512]{3,2,1,0:T(8,128)S(1)}, f32[8,1,8,512]{3,2,1,0:T(8,128)}, u32[]{:S(2)}) copy-start(f32[8,1,8,512]{3,2,1,0:T(8,128)} %copy-done.8) | copy-start | bytes 393220
Sparse Core Ops, SparseCore 0:
  205.6 55.1 all-reduce.3
  388.2 55.5 all-reduce.5
